TPU v7x, 32 devices: a whole 2x2x4 slice. The times are simulated.
32 devices in a mesh: rows: 16 (over z, y, x), panel: 2 (over core).
Axes of the slice: x: 2, y: 2, z: 4, core: 2. Of those that a mesh axis runs over, the one named last changes fastest.
Arguments:
- adj_tiles: bfloat16 [16, 2, 2, 16, 128, 128], P('rows', 'panel'), may hold values from -0.25 to 0.25
- row_counts: int32 [16, 2, 2], P('rows', 'panel'), may hold values from 1 to 16, as said below
- tile_cols: int32 [16, 2, 2, 16], P('rows', 'panel'), may hold values from 0 to 15, as said below
- start_basis: bfloat16 [64, 4096], P(None, ('rows', 'panel')), may hold values from -100 to 100
- start_resid: bfloat16 [64, 4096], P(None, ('rows', 'panel')), may hold values from -100 to 100
- start_search: bfloat16 [64, 4096], P(None, ('rows', 'panel')), may hold values from -100 to 100
- ritz_basis: float32 [3, 64, 192], replicated, may hold values from -1 to 1.5
- ritz_search: float32 [3, 64, 128], replicated, may hold values from -1 to 1.5
Outputs:
- eigvectors: float32 [64, 4096], P(None, ('rows', 'panel'))
- residual: float32 [64, 4096], P(None, ('rows', 'panel'))
- directions: float32 [64, 4096], P(None, ('rows', 'panel'))
- rayleigh: float32 [64, 64], replicated
Inputs may be any that keep to these rules, and one draw needn't show every extreme that they name: `row_counts`: each device's row blocks have 1 to 16 live slots, the live ones first; on one device every row block has 16. `tile_cols`: the live slots of one row block name distinct column blocks.
All inputs are finite; a program needn't handle non-finite values.
Results may differ from a plain program's by a relative error of at most 0.0053.
Values may be sent and summed in bfloat16 or wider, within the bound.
No kernel may reach another device: no remote copies, remote signals or barrier semaphores. Data moves between devices by JAX's collectives and lax.ppermute only.
A program may use at most 64 MiB of HBM per device.

v0:
```python
import jax
import jax.numpy as jnp
from jax import lax
from jax.sharding import PartitionSpec as P

epsilon = 1e-06
highest = lax.Precision.HIGHEST


def lower_solve(factor, values):
    return jax.scipy.linalg.solve_triangular(factor, values, lower=True)


def slot_product(gathered, tile_set, counts, columns):
    vec_rows = gathered.shape[0]
    tile_edge = tile_set.shape[2]
    blocks = gathered.reshape(vec_rows, gathered.shape[1] // tile_edge, tile_edge)
    slot_ids = jnp.arange(tile_set.shape[1], dtype=jnp.int32)
    in_use = slot_ids[None, :] < counts[:, None]
    chosen = jnp.take(blocks, columns.reshape(-1), axis=1)
    chosen = chosen.reshape(vec_rows, columns.shape[0], columns.shape[1], tile_edge)
    chosen = jnp.where(in_use[None, :, :, None], chosen, jnp.zeros((), chosen.dtype))
    summed = jnp.einsum("wbjk,bjik->wbi", chosen, tile_set, preferred_element_type=jnp.float32)
    return summed.reshape(vec_rows, -1)


def body(
    adj_tiles,
    row_counts,
    tile_cols,
    start_basis,
    start_resid,
    start_search,
    ritz_basis,
    ritz_search,
):
    tile_set = adj_tiles[0, 0]
    counts = row_counts[0, 0]
    columns = tile_cols[0, 0]
    vec_count = start_basis.shape[0]
    node_total = start_basis.shape[1] * lax.axis_size("rows") * lax.axis_size("panel")
    basis_b, resid_b, search_b = (start_basis, start_resid, start_search)
    for sweep in range(ritz_basis.shape[0]):
        stacked = jnp.concatenate([basis_b, resid_b, search_b], axis=0)
        stacked_all = lax.all_gather(stacked, "rows", axis=1, tiled=True)
        partial_value = slot_product(stacked_all, tile_set, counts, columns)
        product_rows = lax.psum_scatter(partial_value, "panel", scatter_dimension=1, tiled=True)
        stack_f32 = stacked.astype(jnp.float32)
        image_f32 = stack_f32 - product_rows
        mixing = ritz_basis[sweep]
        search_mix = ritz_search[sweep]
        rotated = jnp.dot(mixing, stack_f32, precision=highest)
        rotated_image = jnp.dot(mixing, image_f32, precision=highest)
        search_raw = jnp.dot(search_mix, stack_f32[vec_count:], precision=highest)
        gram_sum, curve_sum, search_sum = lax.psum(
            (
                jnp.dot(rotated, rotated.T, precision=highest),
                jnp.dot(rotated, rotated_image.T, precision=highest),
                jnp.sum(search_raw * search_raw, axis=1),
            ),
            ("rows", "panel"),
        )
        factor = jnp.linalg.cholesky(gram_sum / node_total)
        basis = lower_solve(factor, rotated)
        basis_image = lower_solve(factor, rotated_image)
        rayleigh = lower_solve(factor, lower_solve(factor, curve_sum / node_total).T).T
        resid_raw = basis_image - jnp.dot(rayleigh.T, basis, precision=highest)
        search_sq = search_sum / node_total
        resid_sq = lax.psum(jnp.sum(resid_raw * resid_raw, axis=1), ("rows", "panel")) / node_total
        resid = resid_raw / jnp.sqrt(resid_sq + epsilon)[:, None]
        search = search_raw / jnp.sqrt(search_sq + epsilon)[:, None]
        basis_b = basis.astype(jnp.bfloat16)
        resid_b = resid.astype(jnp.bfloat16)
        search_b = search.astype(jnp.bfloat16)
    return (basis, resid, search, rayleigh)


def solution(mesh):
    return jax.shard_map(
        body,
        mesh=mesh,
        in_specs=(
            P("rows", "panel", None, None, None, None),
            P("rows", "panel", None),
            P("rows", "panel", None, None),
            P(None, ("rows", "panel")),
            P(None, ("rows", "panel")),
            P(None, ("rows", "panel")),
            P(),
            P(),
        ),
        out_specs=(
            P(None, ("rows", "panel")),
            P(None, ("rows", "panel")),
            P(None, ("rows", "panel")),
            P(),
        ),
        check_vma=False,
    )
```

profile of v0, /device:TPU:0, one launch (start us, length us, event | category | flops | bytes accessed | tf_op | source)
XLA Modules:
  0.0 463.8 jit_solution(4816201861021060135)
XLA Ops:
  7.2 0.8 reshape_squeeze.2
  8.1 0.7 constant_dynamic-update-slice_fusion.2
  8.8 0.7 constant_dynamic-update-slice_fusion.1
  9.5 0.7 constant_dynamic-update-slice_fusion
  10.3 47.0 %all_gather.9 = bf16[192,2048]{1,0:T(8,128)(2,1)S(1)} all-gather(bf16[192,128]{1,0:T(8,128)(2,1)S(1)} %constant_dynamic-update-slice_fusion), channel_id=1, replica_groups=mesh['rows'=16,'panel'=2] {'rows'}, dimensions={1}, use_global_device_ids=true | all-gather | bytes 835584 | tf_op jit(solution)/shard_map/all_gather | solution.py:45
  57.6 0.8 gather_fusion
  58.7 0.6 fusion.9
  59.3 0.7 copy.75
  60.3 1.0 multiply_reduce_fusion.4
  61.5 2.1 reduce-scatter.4.cloned.1.call-done
  63.6 1.1 fusion.30
  64.9 41.0 %all-reduce.5 = (f32[64,64]{0,1:T(8,128)S(1)}, f32[64,64]{0,1:T(8,128)S(1)}) all-reduce(f32[64,64]{0,1:T(8,128)S(1)} %fusion.122, f32[64,64]{0,1:T(8,128)S(1)} %fusion.123), channel_id=1, replica_groups=mesh['rows'=16,'panel'=2] {'rows','panel'}, use_global_device_ids=true, to_apply=%region_0.1 | all-reduce | flops 8192 | bytes 65536 | tf_op jit(solution)/shard_map/psum | solution.py:55
  106.1 5.8 %cholesky.59 = f32[64,64]{1,0:T(8,128)S(1)} custom-call(f32[64,64]{1,0:T(8,128)S(1)} %fusion.95), custom_call_target="Cholesky" | custom-call | tf_op jit(solution)/shard_map/jit(cholesky)/cholesky | solution.py:63
  112.0 0.6 compare_reduce_fusion.2
  112.6 0.7 fusion.48
  113.3 4.9 %custom-call.18 = f32[1,64,64]{1,2,0:T(8,128)S(1)} custom-call(f32[1,64,64]{2,1,0:T(8,128)S(1)} %fusion.48), custom_call_target="InvertDiagBlocksLowerTriangular" | custom-call | tf_op jit(solution)/shard_map/jit(_solve_triangular)/triangular_solve | solution.py:11
  119.1 0.3 multiply_reduce_fusion.5
  119.4 40.0 %all-reduce.4 = (f32[64]{0:T(128)S(1)}, f32[64]{0:T(128)S(1)}) all-reduce(f32[64]{0:T(128)S(1)} %get-tuple-element.32, f32[64]{0:T(128)S(1)} %get-tuple-element.34), channel_id=1, replica_groups=mesh['rows'=16,'panel'=2] {'rows','panel'}, use_global_device_ids=true, to_apply=%region_8.13 | all-reduce | flops 128 | bytes 1024 | tf_op jit(solution)/shard_map/psum | solution.py:55
  159.9 45.3 %all_gather.10 = bf16[192,2048]{1,0:T(8,128)(2,1)S(1)} all-gather(bf16[192,128]{1,0:T(8,128)(2,1)S(1)} %pad_maximum_fusion), channel_id=1, replica_groups=mesh['rows'=16,'panel'=2] {'rows'}, dimensions={1}, use_global_device_ids=true | all-gather | bytes 835584 | tf_op jit(solution)/shard_map/all_gather | solution.py:45
  205.3 0.9 gather_fusion.1
  206.4 0.6 fusion.12
  207.0 0.7 copy.74
  207.8 1.0 multiply_reduce_fusion.2
  209.0 2.3 reduce-scatter.6.cloned.1.call-done
  211.3 1.1 fusion.27
  212.7 41.0 %all-reduce.3 = (f32[64,64]{0,1:T(8,128)S(1)}, f32[64,64]{0,1:T(8,128)S(1)}) all-reduce(f32[64,64]{0,1:T(8,128)S(1)} %fusion.124, f32[64,64]{0,1:T(8,128)S(1)} %fusion.125), channel_id=1, replica_groups=mesh['rows'=16,'panel'=2] {'rows','panel'}, use_global_device_ids=true, to_apply=%region_9.14 | all-reduce | flops 8192 | bytes 65536 | tf_op jit(solution)/shard_map/psum | solution.py:55
  253.8 5.8 %cholesky.70 = f32[64,64]{1,0:T(8,128)S(1)} custom-call(f32[64,64]{1,0:T(8,128)S(1)} %fusion.84), custom_call_target="Cholesky" | custom-call | tf_op jit(solution)/shard_map/jit(cholesky)/cholesky | solution.py:63
  259.7 0.6 compare_reduce_fusion.1
  260.3 0.7 fusion.49
  261.0 4.9 %custom-call.22 = f32[1,64,64]{1,2,0:T(8,128)S(1)} custom-call(f32[1,64,64]{2,1,0:T(8,128)S(1)} %fusion.49), custom_call_target="InvertDiagBlocksLowerTriangular" | custom-call | tf_op jit(solution)/shard_map/jit(_solve_triangular)/triangular_solve | solution.py:11
  266.9 0.3 multiply_reduce_fusion.3
  267.1 40.1 %all-reduce.2 = (f32[64]{0:T(128)S(1)}, f32[64]{0:T(128)S(1)}) all-reduce(f32[64]{0:T(128)S(1)} %get-tuple-element.36, f32[64]{0:T(128)S(1)} %get-tuple-element.40), channel_id=1, replica_groups=mesh['rows'=16,'panel'=2] {'rows','panel'}, use_global_device_ids=true, to_apply=%region_15.20 | all-reduce | flops 128 | bytes 1024 | tf_op jit(solution)/shard_map/psum | solution.py:55
  307.6 45.4 %all_gather.11 = bf16[192,2048]{1,0:T(8,128)(2,1)S(1)} all-gather(bf16[192,128]{1,0:T(8,128)(2,1)S(1)} %pad_maximum_fusion.1), channel_id=1, replica_groups=mesh['rows'=16,'panel'=2] {'rows'}, dimensions={1}, use_global_device_ids=true | all-gather | bytes 835584 | tf_op jit(solution)/shard_map/all_gather | solution.py:45
  353.3 0.9 gather_fusion.2
  354.3 0.6 fusion.15
  355.0 0.7 copy.73
  355.7 1.0 multiply_reduce_fusion
  356.9 2.4 reduce-scatter.8.cloned.1.call-done
  359.3 1.1 fusion.24
  360.6 41.0 %all-reduce.1 = (f32[64,64]{0,1:T(8,128)S(1)}, f32[64,64]{0,1:T(8,128)S(1)}) all-reduce(f32[64,64]{0,1:T(8,128)S(1)} %fusion.126, f32[64,64]{0,1:T(8,128)S(1)} %fusion.127), channel_id=1, replica_groups=mesh['rows'=16,'panel'=2] {'rows','panel'}, use_global_device_ids=true, to_apply=%region_16.21 | all-reduce | flops 8192 | bytes 65536 | tf_op jit(solution)/shard_map/psum | solution.py:55
  401.7 5.8 %cholesky.81 = f32[64,64]{1,0:T(8,128)S(1)} custom-call(f32[64,64]{1,0:T(8,128)S(1)} %fusion.73), custom_call_target="Cholesky" | custom-call | tf_op jit(solution)/shard_map/jit(cholesky)/cholesky | solution.py:63
  407.6 0.6 compare_reduce_fusion
  408.3 0.7 fusion.50
  408.9 4.9 %custom-call.26 = f32[1,64,64]{1,2,0:T(8,128)S(1)} custom-call(f32[1,64,64]{2,1,0:T(8,128)S(1)} %fusion.50), custom_call_target="InvertDiagBlocksLowerTriangular" | custom-call | tf_op jit(solution)/shard_map/jit(_solve_triangular)/triangular_solve | solution.py:11
  415.1 40.1 %all-reduce = (f32[64]{0:T(128)S(1)}, f32[64]{0:T(128)S(1)}) all-reduce(f32[64]{0:T(128)S(1)} %get-tuple-element.44, f32[64]{0:T(128)S(1)} %get-tuple-element.46), channel_id=1, replica_groups=mesh['rows'=16,'panel'=2] {'rows','panel'}, use_global_device_ids=true, to_apply=%region_20.25 | all-reduce | flops 128 | bytes 1024 | tf_op jit(solution)/shard_map/psum | solution.py:69
  455.2 0.7 copy.51
  455.9 0.7 divide_bitcast_fusion
  456.6 0.7 broadcast_divide_fusion
  (75 shorter events, 7.1 us)
Async XLA Ops:
  7.2 51.5 %copy-start = (bf16[1,1,2,16,128,128]{5,4,3,2,1,0:T(8,128)(2,1)S(1)}, bf16[1,1,2,16,128,128]{5,4,3,2,1,0:T(8,128)(2,1)}, u32[]{:S(2)}) copy-start(bf16[1,1,2,16,128,128]{5,4,3,2,1,0:T(8,128)(2,1)} %param.15) | copy-start | bytes 3145732
  7.2 50.3 %copy-start.6 = (s32[1,1,2]{2,1,0:T(1,128)S(1)}, s32[1,1,2]{2,1,0:T(1,128)}, u32[]{:S(2)}) copy-start(s32[1,1,2]{2,1,0:T(1,128)} %param.16) | copy-start | bytes 28
  7.2 56.4 %reduce-scatter.4.cloned.1.call-start = ((), (), s32[]{:S(2)}) async-start(), calls=%async_computation.3 | async-start | bytes 294912 | tf_op jit(solution)/shard_map/reduce_scatter | solution.py:47
  58.6 1.4 copy-start.1
  58.7 1.6 copy-start.4
  58.7 1.6 copy-start.5
  60.0 151.3 %reduce-scatter.6.cloned.1.call-start = ((), (), s32[]{:S(2)}) async-start(), calls=%async_computation.4 | async-start | bytes 294912 | tf_op jit(solution)/shard_map/reduce_scatter | solution.py:47
  206.4 4.9 %copy-start.2 = (f32[3,64,192]{2,1,0:T(8,128)S(1)}, f32[3,64,192]{2,1,0:T(8,128)}, u32[]{:S(2)}) copy-start(f32[3,64,192]{2,1,0:T(8,128)} %param.21) | copy-start | bytes 442372
  207.7 151.5 %reduce-scatter.8.cloned.1.call-start = ((), (), s32[]{:S(2)}) async-start(), calls=%async_computation.5 | async-start | bytes 294912 | tf_op jit(solution)/shard_map/reduce_scatter | solution.py:47
  414.3 43.0 %copy-start.3 = (f32[64,128]{1,0:T(8,128)}, f32[64,128]{1,0:T(8,128)S(1)}, u32[]{:S(2)}) copy-start(f32[64,128]{1,0:T(8,128)S(1)} %fusion.66) | copy-start | bytes 98308
Sparse Core Ops, SparseCore 0:
  60.1 3.4 reduce-scatter.3
  207.9 3.4 reduce-scatter.5
  355.8 3.4 reduce-scatter.7
where the time goes:
time: 465 us; the launch traced here: 464 us
  blocking collectives  381 us (82%)
  other arithmetic  38.8 us (8%)
  between operations  14.3 us (3%)
  matrix products  13.6 us (3%)
  local copies, waits for them, and re-layouts  9.17 us (2%)
  waiting for transfers between devices  6.79 us (1%)
    psum x5, blocking collectives, body(): lax.psum((jnp.dot(rotated, rotated.T, precision=highest), jnp.dot(rotated...  203 us
    all_gather x3, blocking collectives, body(): stacked_all = lax.all_gather(stacked, 'rows', axis=1, tiled=True)  138 us
    psum x1, blocking collectives, body(): lax.psum(jnp.sum(resid_raw * resid_raw, axis=1), ('rows', 'panel'))  40.1 us
    another operation x9, other arithmetic, body(): factor = jnp.linalg.cholesky(gram_sum / node_total)  19.6 us
    another operation x6, other arithmetic, lower_solve(): return jax.scipy.linalg.solve_triangular(factor, values, lower=True)  16.6 us
  transfers between devices with their start and end apart: 3, of which 3 were waited for; matrix products, arithmetic and copies ran while one was open for 1% of the time, Pallas kernels for 0%

commit v1 on v0

--- a/solution.py
+++ b/solution.py
@@ -66,7 +66,12 @@
         rayleigh = lower_solve(factor, lower_solve(factor, curve_sum / node_total).T).T
         resid_raw = basis_image - jnp.dot(rayleigh.T, basis, precision=highest)
         search_sq = search_sum / node_total
-        resid_sq = lax.psum(jnp.sum(resid_raw * resid_raw, axis=1), ("rows", "panel")) / node_total
+        resid_sq = (
+            jnp.sum(
+                lax.all_gather(jnp.sum(resid_raw * resid_raw, axis=1), ("rows", "panel")), axis=0
+            )
+            / node_total
+        )
         resid = resid_raw / jnp.sqrt(resid_sq + epsilon)[:, None]
         search = search_raw / jnp.sqrt(search_sq + epsilon)[:, None]
         basis_b = basis.astype(jnp.bfloat16)

time: 465 us -> 467 us (level)
    unnamed x0 -> x1, blocking collectives: none -> 40.3 us
    psum x1 -> x0, blocking collectives: 40.1 us -> none  [body(): lax.psum(jnp.sum(resid_raw * resid_raw, axis=1), ('rows', 'panel'))]
where the time goes in v1:
time: 467 us; the launch traced here: 465 us
  blocking collectives  381 us (82%)
  other arithmetic  38.9 us (8%)
  between operations  14.4 us (3%)
  matrix products  13.6 us (3%)
  local copies, waits for them, and re-layouts  10.2 us (2%)
  waiting for transfers between devices  6.77 us (1%)
    psum x5, blocking collectives, body(): lax.psum((jnp.dot(rotated, rotated.T, precision=highest), jnp.dot(rotated...  204 us
    all_gather x3, blocking collectives, body(): stacked_all = lax.all_gather(stacked, 'rows', axis=1, tiled=True)  138 us
    unnamed x1, blocking collectives  40.3 us
    another operation x9, other arithmetic, body(): factor = jnp.linalg.cholesky(gram_sum / node_total)  19.6 us
    another operation x6, other arithmetic, lower_solve(): return jax.scipy.linalg.solve_triangular(factor, values, lower=True)  16.6 us
  transfers between devices with their start and end apart: 3, of which 3 were waited for; matrix products, arithmetic and copies ran while one was open for 1% of the time, Pallas kernels for 0%

profile of v1, /device:TPU:0, one launch (start us, length us, event | category | flops | bytes accessed | tf_op | source)
XLA Modules:
  0.0 465.3 jit_solution(14981475848559828143)
XLA Ops:
  7.2 0.8 reshape_squeeze.2
  8.1 0.7 constant_dynamic-update-slice_fusion.2
  8.8 0.7 constant_dynamic-update-slice_fusion.1
  9.5 0.7 constant_dynamic-update-slice_fusion
  10.3 47.0 %all_gather.27 = bf16[192,2048]{1,0:T(8,128)(2,1)S(1)} all-gather(bf16[192,128]{1,0:T(8,128)(2,1)S(1)} %constant_dynamic-update-slice_fusion), channel_id=1, replica_groups=mesh['rows'=16,'panel'=2] {'rows'}, dimensions={1}, use_global_device_ids=true | all-gather | bytes 835584 | tf_op jit(solution)/shard_map/all_gather | solution.py:45
  57.6 0.8 gather_fusion
  58.7 0.6 fusion.9
  59.3 0.7 copy.91
  60.3 1.0 multiply_reduce_fusion.4
  61.5 2.1 reduce-scatter.4.cloned.1.call-done
  63.6 1.1 fusion.30
  64.9 41.0 %all-reduce.8 = (f32[64,64]{0,1:T(8,128)S(1)}, f32[64,64]{0,1:T(8,128)S(1)}) all-reduce(f32[64,64]{0,1:T(8,128)S(1)} %fusion.122, f32[64,64]{0,1:T(8,128)S(1)} %fusion.123), channel_id=1, replica_groups=mesh['rows'=16,'panel'=2] {'rows','panel'}, use_global_device_ids=true, to_apply=%region_0.1 | all-reduce | flops 8192 | bytes 65536 | tf_op jit(solution)/shard_map/psum | solution.py:55
  106.1 5.8 %cholesky.59 = f32[64,64]{1,0:T(8,128)S(1)} custom-call(f32[64,64]{1,0:T(8,128)S(1)} %fusion.95), custom_call_target="Cholesky" | custom-call | tf_op jit(solution)/shard_map/jit(cholesky)/cholesky | solution.py:63
  112.0 0.6 compare_reduce_fusion.2
  112.6 0.7 fusion.48
  113.3 4.9 %custom-call.18 = f32[1,64,64]{1,2,0:T(8,128)S(1)} custom-call(f32[1,64,64]{2,1,0:T(8,128)S(1)} %fusion.48), custom_call_target="InvertDiagBlocksLowerTriangular" | custom-call | tf_op jit(solution)/shard_map/jit(_solve_triangular)/triangular_solve | solution.py:11
  119.4 0.3 dynamic-update-slice.2
  119.7 40.1 %all-reduce.7 = (f32[64]{0:T(128)S(1)}, f32[2048]{0:T(1024)S(1)}) all-reduce(f32[64]{0:T(128)S(1)} %get-tuple-element.36, f32[2048]{0:T(1024)S(1)} %dynamic-update-slice.2), channel_id=1, replica_groups=mesh['rows'=16,'panel'=2] {'rows','panel'}, use_global_device_ids=true, to_apply=%region_8.13 | all-reduce | flops 2112 | bytes 16896 | tf_op jit(solution)/shard_map/psum | solution.py:55
  160.3 45.3 %all_gather.30 = bf16[192,2048]{1,0:T(8,128)(2,1)S(1)} all-gather(bf16[192,128]{1,0:T(8,128)(2,1)S(1)} %pad_maximum_fusion), channel_id=1, replica_groups=mesh['rows'=16,'panel'=2] {'rows'}, dimensions={1}, use_global_device_ids=true | all-gather | bytes 835584 | tf_op jit(solution)/shard_map/all_gather | solution.py:45
  205.8 0.9 gather_fusion.1
  206.9 0.6 fusion.12
  207.5 0.7 copy.90
  208.2 1.0 multiply_reduce_fusion.2
  209.5 2.3 reduce-scatter.6.cloned.1.call-done
  211.8 1.1 fusion.27
  213.1 41.0 %all-reduce.6 = (f32[64,64]{0,1:T(8,128)S(1)}, f32[64,64]{0,1:T(8,128)S(1)}) all-reduce(f32[64,64]{0,1:T(8,128)S(1)} %fusion.124, f32[64,64]{0,1:T(8,128)S(1)} %fusion.125), channel_id=1, replica_groups=mesh['rows'=16,'panel'=2] {'rows','panel'}, use_global_device_ids=true, to_apply=%region_9.14 | all-reduce | flops 8192 | bytes 65536 | tf_op jit(solution)/shard_map/psum | solution.py:55
  254.2 5.8 %cholesky.70 = f32[64,64]{1,0:T(8,128)S(1)} custom-call(f32[64,64]{1,0:T(8,128)S(1)} %fusion.84), custom_call_target="Cholesky" | custom-call | tf_op jit(solution)/shard_map/jit(cholesky)/cholesky | solution.py:63
  260.1 0.6 compare_reduce_fusion.1
  260.8 0.7 fusion.49
  261.4 4.9 %custom-call.22 = f32[1,64,64]{1,2,0:T(8,128)S(1)} custom-call(f32[1,64,64]{2,1,0:T(8,128)S(1)} %fusion.49), custom_call_target="InvertDiagBlocksLowerTriangular" | custom-call | tf_op jit(solution)/shard_map/jit(_solve_triangular)/triangular_solve | solution.py:11
  267.6 0.3 dynamic-update-slice.3
  267.9 40.3 %all-reduce.5 = (f32[64]{0:T(128)S(1)}, f32[2048]{0:T(1024)S(1)}) all-reduce(f32[64]{0:T(128)S(1)} %get-tuple-element.40, f32[2048]{0:T(1024)S(1)} %dynamic-update-slice.3), channel_id=1, replica_groups=mesh['rows'=16,'panel'=2] {'rows','panel'}, use_global_device_ids=true, to_apply=%region_15.20 | all-reduce | flops 2112 | bytes 16896 | tf_op jit(solution)/shard_map/psum | solution.py:55
  308.7 45.3 %all_gather.33 = bf16[192,2048]{1,0:T(8,128)(2,1)S(1)} all-gather(bf16[192,128]{1,0:T(8,128)(2,1)S(1)} %pad_maximum_fusion.1), channel_id=1, replica_groups=mesh['rows'=16,'panel'=2] {'rows'}, dimensions={1}, use_global_device_ids=true | all-gather | bytes 835584 | tf_op jit(solution)/shard_map/all_gather | solution.py:45
  354.2 0.9 gather_fusion.2
  355.2 0.6 fusion.15
  355.9 0.7 copy.89
  356.6 1.0 multiply_reduce_fusion
  357.8 2.4 reduce-scatter.8.cloned.1.call-done
  360.2 1.1 fusion.24
  361.5 41.0 %all-reduce.4 = (f32[64,64]{0,1:T(8,128)S(1)}, f32[64,64]{0,1:T(8,128)S(1)}) all-reduce(f32[64,64]{0,1:T(8,128)S(1)} %fusion.126, f32[64,64]{0,1:T(8,128)S(1)} %fusion.127), channel_id=1, replica_groups=mesh['rows'=16,'panel'=2] {'rows','panel'}, use_global_device_ids=true, to_apply=%region_16.21 | all-reduce | flops 8192 | bytes 65536 | tf_op jit(solution)/shard_map/psum | solution.py:55
  402.6 5.8 %cholesky.81 = f32[64,64]{1,0:T(8,128)S(1)} custom-call(f32[64,64]{1,0:T(8,128)S(1)} %fusion.73), custom_call_target="Cholesky" | custom-call | tf_op jit(solution)/shard_map/jit(cholesky)/cholesky | solution.py:63
  408.5 0.6 compare_reduce_fusion
  409.1 0.7 fusion.50
  409.8 4.9 %custom-call.26 = f32[1,64,64]{1,2,0:T(8,128)S(1)} custom-call(f32[1,64,64]{2,1,0:T(8,128)S(1)} %fusion.50), custom_call_target="InvertDiagBlocksLowerTriangular" | custom-call | tf_op jit(solution)/shard_map/jit(_solve_triangular)/triangular_solve | solution.py:11
  416.2 40.3 %all-reduce.3 = (f32[2048]{0:T(1024)S(1)}, f32[64]{0:T(128)S(1)}) all-reduce(f32[2048]{0:T(1024)S(1)} %dynamic-update-slice.4, f32[64]{0:T(128)S(1)} %get-tuple-element.50), channel_id=4, replica_groups=mesh['rows'=16,'panel'=2] {'rows','panel'}, use_global_device_ids=true, to_apply=%add.2 | all-reduce | flops 2112 | bytes 16896
  456.6 0.7 copy.67
  457.3 0.7 divide_bitcast_fusion
  458.0 0.7 broadcast_divide_fusion
  (88 shorter events, 8.2 us)
Async XLA Ops:
  7.2 51.5 %copy-start = (bf16[1,1,2,16,128,128]{5,4,3,2,1,0:T(8,128)(2,1)S(1)}, bf16[1,1,2,16,128,128]{5,4,3,2,1,0:T(8,128)(2,1)}, u32[]{:S(2)}) copy-start(bf16[1,1,2,16,128,128]{5,4,3,2,1,0:T(8,128)(2,1)} %param.15) | copy-start | bytes 3145732
  7.2 50.3 %copy-start.6 = (s32[1,1,2]{2,1,0:T(1,128)S(1)}, s32[1,1,2]{2,1,0:T(1,128)}, u32[]{:S(2)}) copy-start(s32[1,1,2]{2,1,0:T(1,128)} %param.16) | copy-start | bytes 28
  7.2 56.4 %reduce-scatter.4.cloned.1.call-start = ((), (), s32[]{:S(2)}) async-start(), calls=%async_computation.3 | async-start | bytes 294912 | tf_op jit(solution)/shard_map/reduce_scatter | solution.py:47
  58.6 1.4 copy-start.1
  58.7 1.6 copy-start.4
  58.7 1.6 copy-start.5
  60.0 151.8 %reduce-scatter.6.cloned.1.call-start = ((), (), s32[]{:S(2)}) async-start(), calls=%async_computation.4 | async-start | bytes 294912 | tf_op jit(solution)/shard_map/reduce_scatter | solution.py:47
  206.8 4.9 %copy-start.2 = (f32[3,64,192]{2,1,0:T(8,128)S(1)}, f32[3,64,192]{2,1,0:T(8,128)}, u32[]{:S(2)}) copy-start(f32[3,64,192]{2,1,0:T(8,128)} %param.21) | copy-start | bytes 442372
  208.2 152.0 %reduce-scatter.8.cloned.1.call-start = ((), (), s32[]{:S(2)}) async-start(), calls=%async_computation.5 | async-start | bytes 294912 | tf_op jit(solution)/shard_map/reduce_scatter | solution.py:47
  415.2 43.5 %copy-start.3 = (f32[64,128]{1,0:T(8,128)}, f32[64,128]{1,0:T(8,128)S(1)}, u32[]{:S(2)}) copy-start(f32[64,128]{1,0:T(8,128)S(1)} %fusion.66) | copy-start | bytes 98308
Sparse Core Ops, SparseCore 0:
  60.1 3.4 reduce-scatter.3
  208.3 3.4 reduce-scatter.5
  356.7 3.4 reduce-scatter.7
